TPU v7x, 32 devices: a whole 2x2x4 slice. The times are simulated.
32 devices in a mesh: cg: 8 (over z, x), vg: 4 (over y, core).
Axes of the slice: x: 2, y: 2, z: 4, core: 2. Of those that a mesh axis runs over, the one named last changes fastest.
Arguments:
- con_embed: float32 [32768, 128], P(('cg', 'vg')), may hold values from -6 to 6
- var_embed: float32 [32768, 128], P(('vg', 'cg')), may hold values from -6 to 6
- row_coef: float32 [32768], P(('cg', 'vg')), may hold values from 0.3 to 3
- col_coef: float32 [32768], P(('vg', 'cg')), may hold values from 0.3 to 3
- self_weight: float32 [128, 128], replicated, may hold values from -0.5 to 0.5
- msg_weight: float32 [128, 128], replicated, may hold values from -0.0234375 to 0.0234375
- timestep: int32 [1], replicated, may hold values from 0 to 999
- tile_rows: int32 [8, 4, 16], P('cg', 'vg'), may hold values from 0 to 7, as said below
- tile_cols: int32 [8, 4, 16], P('cg', 'vg'), may hold values from 0 to 15, as said below
- pattern: bfloat16 [8, 4, 16, 512, 512], P('cg', 'vg'), may hold values from -6 to 6
- cotangent: float32 [32768, 128], P(('cg', 'vg')), may hold values from -6 to 6
Outputs:
- con_update: float32 [32768, 128], P(('cg', 'vg'))
- grad_con: float32 [32768, 128], P(('cg', 'vg'))
- grad_var: float32 [32768, 128], P(('vg', 'cg'))
- grad_msg: float32 [128, 128], replicated
- grad_self: float32 [128, 128], replicated
Inputs may be any that keep to these rules, and one draw needn't show every extreme that they name: `tile_rows`: every device lists tile row 0 and tile row 7; a device lists distinct tiles unless 16 exceeds 8 * 16, and repeated tiles add. `tile_cols`: every device lists tile column 0 and tile column 15, together with the rows above: tiles (0, 0) and (7, 15) are on every list.
All inputs are finite; a program needn't handle non-finite values.
Results may differ from a plain program's by a relative error of at most 0.007.
Values may be sent and summed in bfloat16 or wider, within the bound.
A program may use at most 128 MiB of HBM per device.

v0:
```python
import math
import jax
import jax.numpy as jnp
from jax import lax
from jax.sharding import PartitionSpec as P

H = 128
TB = 512


def body(
    con_embed,
    var_embed,
    row_coef,
    col_coef,
    self_weight,
    msg_weight,
    timestep,
    tile_rows,
    tile_cols,
    pattern,
    cotangent,
):
    highest = lax.Precision.HIGHEST
    con_count = con_embed.shape[0]
    var_count = var_embed.shape[0]
    row_blocks = con_count * lax.axis_size("vg") // TB
    col_blocks = var_count * lax.axis_size("cg") // TB
    row_index = tile_rows.reshape(-1)
    col_index = tile_cols.reshape(-1)
    tile_count = row_index.shape[0]
    per_turn = math.gcd(tile_count, 8)
    turns = tile_count // per_turn
    patterns_here = pattern.reshape(turns, per_turn, TB, TB)
    row_turns = row_index.reshape(turns, per_turn)
    col_turns = col_index.reshape(turns, per_turn)
    local_proj = (
        jnp.dot(var_embed, msg_weight, precision=highest, preferred_element_type=jnp.float32)
        * col_coef[:, None]
    ).astype(jnp.bfloat16)
    projected = lax.all_gather(local_proj, "cg", axis=0, tiled=True)
    source_blocks = projected.reshape(col_blocks, TB, H)
    row_ids = jnp.arange(row_blocks, dtype=jnp.int32)
    col_ids = jnp.arange(col_blocks, dtype=jnp.int32)

    def forward_turn(running, inputs):
        rows_now, cols_now, tile_mask = inputs
        products = jnp.einsum(
            "grc,gch->grh", tile_mask, source_blocks[cols_now], preferred_element_type=jnp.float32
        )
        selector = (rows_now[None, :] == row_ids[:, None]).astype(jnp.float32)
        running = running + jnp.dot(
            selector,
            products.reshape(per_turn, TB * H),
            precision=highest,
            preferred_element_type=jnp.float32,
        )
        return (running, None)

    forward_sum, _ = lax.scan(
        forward_turn,
        jnp.zeros((row_blocks, TB * H), jnp.float32),
        (row_turns, col_turns, patterns_here),
    )
    messages = lax.psum_scatter(
        forward_sum.reshape(row_blocks * TB, H), "vg", scatter_dimension=0, tiled=True
    )
    frequency = jnp.exp(-math.log(10000.0) * jnp.arange(H // 2, dtype=jnp.float32) / (H // 2))
    phases = timestep[0].astype(jnp.float32) * frequency
    time_embed = jnp.concatenate([jnp.sin(phases), jnp.cos(phases)])
    preact = (
        jnp.dot(con_embed, self_weight, precision=highest, preferred_element_type=jnp.float32)
        + row_coef[:, None] * messages
        + time_embed[None, :]
    )
    sigmoid_z = jax.nn.sigmoid(preact)
    con_update = con_embed + preact * sigmoid_z
    grad_pre = cotangent * sigmoid_z * (1.0 + preact * (1.0 - sigmoid_z))
    grad_con = cotangent + jnp.dot(
        grad_pre, self_weight.T, precision=highest, preferred_element_type=jnp.float32
    )
    local_self = jnp.dot(
        con_embed.T, grad_pre, precision=highest, preferred_element_type=jnp.float32
    )
    grad_messages = (row_coef[:, None] * grad_pre).astype(jnp.bfloat16)
    whole_rows = lax.all_gather(grad_messages, "vg", axis=0, tiled=True).reshape(row_blocks, TB, H)

    def backward_turn(running, inputs):
        rows_now, cols_now, tile_mask = inputs
        products = jnp.einsum(
            "grc,grh->gch", tile_mask, whole_rows[rows_now], preferred_element_type=jnp.float32
        )
        selector = (cols_now[None, :] == col_ids[:, None]).astype(jnp.float32)
        running = running + jnp.dot(
            selector,
            products.reshape(per_turn, TB * H),
            precision=highest,
            preferred_element_type=jnp.float32,
        )
        return (running, None)

    backward_sum, _ = lax.scan(
        backward_turn,
        jnp.zeros((col_blocks, TB * H), jnp.float32),
        (row_turns, col_turns, patterns_here),
    )
    grad_projected = lax.psum_scatter(
        backward_sum.reshape(col_blocks * TB, H), "cg", scatter_dimension=0, tiled=True
    )
    grad_lin = col_coef[:, None] * grad_projected
    grad_var = jnp.dot(
        grad_lin, msg_weight.T, precision=highest, preferred_element_type=jnp.float32
    )
    local_msg = jnp.dot(
        var_embed.T, grad_lin, precision=highest, preferred_element_type=jnp.float32
    )
    grad_msg, grad_self = lax.psum((local_msg, local_self), ("cg", "vg"))
    return (con_update, grad_con, grad_var, grad_msg, grad_self)


def solution(mesh):
    in_specs = (
        P(("cg", "vg"), None),
        P(("vg", "cg"), None),
        P(("cg", "vg")),
        P(("vg", "cg")),
        P(),
        P(),
        P(),
        P("cg", "vg", None),
        P("cg", "vg", None),
        P("cg", "vg", None, None, None),
        P(("cg", "vg"), None),
    )
    out_specs = (P(("cg", "vg"), None), P(("cg", "vg"), None), P(("vg", "cg"), None), P(), P())
    return jax.shard_map(body, mesh=mesh, in_specs=in_specs, out_specs=out_specs, check_vma=False)
```

profile of v0, /device:TPU:0, one launch (start us, length us, event | category | flops | bytes accessed | tf_op | source)
XLA Modules:
  0.0 396.2 jit_solution(18261910513397852142)
XLA Ops:
  8.2 2.1 fusion.31
  10.9 1.3 reduce.6
  12.3 1.3 reduce.7
  13.7 48.8 %all-gather.3.cloned.1.call-done = bf16[8192,128]{1,0:T(8,128)(2,1)} async-done(((bf16[1024,128]{1,0:T(8,128)(2,1)}), bf16[8192,128]{1,0:T(8,128)(2,1)}) %all-gather.3.cloned.1.call-update) | async-done | bytes 2097168 | tf_op jit(solution)/shard_map/all_gather | solution.py:41
  62.5 22.9 %while.22 = (s32[]{:T(128)}, f32[8,65536]{1,0:T(8,128)}, s32[2,8]{1,0:T(2,128)S(1)}, bf16[2,8,512,512]{3,2,1,0:T(8,128)(2,1)}, s32[2,8]{1,0:T(2,128)S(1)}, /*ind...) while((s32[]{:T(128)}, f32[8,65536]{1,0:T(8,128)}, s32[2,8]{1,0:T(2,128)S(1)}, ...), condition=%wide.region_1.2_spmd.clone, body=%wide.region_0.1_spmd.clone.sunk | while | flops 588252224 | bytes 15733575 | solution.py:60
  62.5 3.2 gather_fusion
  65.8 3.7 fusion.65
  69.5 3.6 convolution_add_fusion.6
  73.2 3.2 gather_fusion
  76.4 3.7 fusion.65
  80.2 5.2 %convolution_add_fusion.6 = f32[8,65536]{1,0:T(8,128)} fusion(f32[1,8,512,128]{3,2,1,0:T(8,128)S(1)} %fusion.65, f32[8,65536]{1,0:T(8,128)} %get-tuple-element.252, pred[]{:T(512)S(6)} %compare.6, s32[8]{0:T(128)S(1)} %fusion.66), kind=kOutput, calls=%fused_computation.4.clone.1 | convolution fusion | flops 51380288 | bytes 6291489 | tf_op jit(solution)/shard_map/while/body/eval_jaxpr/dot_general | solution.py:52
  85.4 3.2 reshape.95
  89.6 28.9 %reduce-scatter.3.cloned.1.call-done = f32[1024,128]{1,0:T(8,128)} async-done(((f32[4096,128]{1,0:T(8,128)}), f32[1024,128]{1,0:T(8,128)}) %reduce-scatter.3.cloned.1.call-update) | async-done | bytes 524304 | tf_op jit(solution)/shard_map/reduce_scatter | solution.py:65
  118.5 2.9 multiply_convert_fusion
  121.5 12.3 %copy.16 = bf16[1,1,16,512,512]{3,4,2,1,0:T(8,128)(2,1)} copy(bf16[1,1,16,512,512]{4,3,2,1,0:T(8,128)(2,1)} %bitcast.88) | data formatting | bytes 16777216 | tf_op args[9]
  133.8 4.5 %all-gather.5.cloned.1.call-done = bf16[4096,128]{1,0:T(8,128)(2,1)} async-done(((bf16[1024,128]{1,0:T(8,128)(2,1)}), bf16[4096,128]{1,0:T(8,128)(2,1)}) %all-gather.5.cloned.1.call-update) | async-done | bytes 1048592 | tf_op jit(solution)/shard_map/all_gather | solution.py:86
  138.3 25.2 %while.23 = (s32[]{:T(128)}, f32[16,65536]{1,0:T(8,128)}, s32[2,8]{1,0:T(2,128)S(1)}, bf16[2,8,512,512]{2,3,1,0:T(8,128)(2,1)}, s32[2,8]{1,0:T(2,128)S(1)}, /*in...) while((s32[]{:T(128)}, f32[16,65536]{1,0:T(8,128)}, s32[2,8]{1,0:T(2,128)S(1)}, ...), condition=%wide.region_4.5_spmd.clone, body=%wide.region_3.4_spmd.clone.sunk | while | flops 639632512 | bytes 19927880 | solution.py:102
  138.3 2.9 gather_fusion.1
  141.2 3.7 fusion.71
  144.9 4.9 %convolution_add_fusion.7 = f32[16,65536]{1,0:T(8,128)} fusion(f32[16,65536]{1,0:T(8,128)} %get-tuple-element.276, f32[1,8,512,128]{3,2,1,0:T(8,128)S(1)} %fusion.71, pred[]{:T(512)S(6)} %compare.7, s32[8]{0:T(128)S(1)} %fusion.72), kind=kOutput, calls=%fused_computation.21.clone.1 | convolution fusion | flops 102760576 | bytes 10485793 | tf_op jit(solution)/shard_map/while/body/eval_jaxpr/dot_general | solution.py:94
  149.8 2.9 gather_fusion.1
  152.7 3.7 fusion.71
  156.5 7.1 %convolution_add_fusion.7 = f32[16,65536]{1,0:T(8,128)} fusion(f32[16,65536]{1,0:T(8,128)} %get-tuple-element.276, f32[1,8,512,128]{3,2,1,0:T(8,128)S(1)} %fusion.71, pred[]{:T(512)S(6)} %compare.7, s32[8]{0:T(128)S(1)} %fusion.72), kind=kOutput, calls=%fused_computation.21.clone.1 | convolution fusion | flops 102760576 | bytes 10485793 | tf_op jit(solution)/shard_map/while/body/eval_jaxpr/dot_general | solution.py:94
  163.5 3.9 reshape.97
  168.6 1.7 convolution_bitcast_fusion
  170.3 1.5 convolution_add_fusion.2
  171.9 84.1 %reduce-scatter.5.cloned.1.call-done = f32[1024,128]{1,0:T(8,128)} async-done(((f32[8192,128]{1,0:T(8,128)}), f32[1024,128]{1,0:T(8,128)}) %reduce-scatter.5.cloned.1.call-update) | async-done | bytes 524304 | tf_op jit(solution)/shard_map/reduce_scatter | solution.py:107
  256.0 2.8 convolution_bitcast_fusion.1
  258.8 2.5 fusion.33
  261.3 125.3 %all-reduce.3.cloned.1.call-done = (f32[128,128]{0,1:T(8,128)}, f32[128,128]{0,1:T(8,128)}) async-done(((f32[128,128]{0,1:T(8,128)}, f32[128,128]{0,1:T(8,128)}), (f32[128,128]{0,1:T(8,128)}, f32[128,128]{0,1:T(8,128)})) %all-reduce.3.cloned.1.call-update) | async-done | bytes 131088 | tf_op jit(solution)/shard_map/psum | solution.py:117
  386.6 1.6 copy.18
  388.1 1.6 copy.19
  (47 shorter events, 3.3 us)
Async XLA Ops:
  7.2 1.0 copy-start
  7.2 55.3 %all-gather.3.cloned.1.call-start = ((), (), s32[]{:S(2)}) async-start(), calls=%async_computation.2 | async-start | bytes 2359296 | tf_op jit(solution)/shard_map/all_gather | solution.py:41
  10.3 108.2 %reduce-scatter.3.cloned.1.call-start = ((), (), s32[]{:S(2)}) async-start(), calls=%async_computation.3 | async-start | bytes 2621440 | tf_op jit(solution)/shard_map/reduce_scatter | solution.py:65
  88.6 29.9 %copy-start.3 = (f32[1024,128]{1,0:T(8,128)S(1)}, f32[1024,128]{1,0:T(8,128)}, u32[]{:S(2)}) copy-start(f32[1024,128]{1,0:T(8,128)} %param.15) | copy-start | bytes 1572868
  88.6 29.9 %copy-start.4 = (f32[1024,128]{1,0:T(8,128)S(1)}, f32[1024,128]{1,0:T(8,128)}, u32[]{:S(2)}) copy-start(f32[1024,128]{1,0:T(8,128)} %param.25) | copy-start | bytes 1572868
  88.6 29.9 %copy-start.6 = (f32[128,128]{1,0:T(8,128)S(1)}, f32[128,128]{1,0:T(8,128)}, u32[]{:S(2)}) copy-start(f32[128,128]{1,0:T(8,128)} %param.19) | copy-start | bytes 196612
  88.6 29.9 %copy-start.7 = (f32[1024]{0:T(1024)S(1)}, f32[1024]{0:T(1024)}, u32[]{:S(2)}) copy-start(f32[1024]{0:T(1024)} %param.17) | copy-start | bytes 12292
  88.7 49.6 %all-gather.5.cloned.1.call-start = ((), (), s32[]{:S(2)}) async-start(), calls=%async_computation.4 | async-start | bytes 1310720 | tf_op jit(solution)/shard_map/all_gather | solution.py:86
  121.4 134.5 %reduce-scatter.5.cloned.1.call-start = ((), (), s32[]{:S(2)}) async-start(), calls=%async_computation.5 | async-start | bytes 4718592 | tf_op jit(solution)/shard_map/reduce_scatter | solution.py:107
  167.4 1.0 copy-start.5
  167.4 1.2 copy-start.8
  167.4 219.2 %all-reduce.3.cloned.1.call-start = ((), (), s32[]{:S(2)}) async-start(), calls=%async_computation.6 | async-start | bytes 262144 | tf_op jit(solution)/shard_map/psum | solution.py:117
  170.3 85.6 %copy-start.2 = (f32[1024]{0:T(1024)S(1)}, f32[1024]{0:T(1024)}, u32[]{:S(2)}) copy-start(f32[1024]{0:T(1024)} %param.18) | copy-start | bytes 12292
  170.3 88.5 %copy-start.1 = (f32[128,128]{1,0:T(8,128)S(1)}, f32[128,128]{1,0:T(8,128)}, u32[]{:S(2)}) copy-start(f32[128,128]{1,0:T(8,128)} %param.20) | copy-start | bytes 196612
Sparse Core Ops, SparseCore 0:
  10.7 51.7 all-gather.2
  88.8 29.6 reduce-scatter.2
  121.5 16.7 all-gather.4
  167.5 88.3 reduce-scatter.4
  262.1 124.4 all-reduce.2
where the time goes:
time: 397 us; the launch traced here: 396 us
  waiting for transfers between devices  292 us (74%)
  matrix products  49.2 us (12%)
  local copies, waits for them, and re-layouts  37.4 us (9%)
  between operations  14.6 us (4%)
    psum x1, waiting for transfers between devices, body(): grad_msg, grad_self = lax.psum((local_msg, local_self), ('cg', 'vg'))  125 us
    reduce_scatter x1, waiting for transfers between devices, body(): lax.psum_scatter(backward_sum.reshape(col_blocks * TB, H), 'cg', scatter_...  84.1 us
    all_gather x1, waiting for transfers between devices, body(): projected = lax.all_gather(local_proj, 'cg', axis=0, tiled=True)  48.8 us
    reduce_scatter x1, waiting for transfers between devices, body(): lax.psum_scatter(forward_sum.reshape(row_blocks * TB, H), 'vg', scatter_d...  28.9 us
    unnamed x22, local copies, waits for them, and re-layouts  17.9 us
    dot_general x2, matrix products, backward_turn(): jnp.dot(selector, products.reshape(per_turn, TB * H), precision=highest,...  12 us
    dot_general x2, matrix products, forward_turn(): jnp.dot(selector, products.reshape(per_turn, TB * H), precision=highest,...  8.83 us
  transfers between devices with their start and end apart: 5, of which 5 were waited for; matrix products, arithmetic and copies ran while one was open for 5% of the time, Pallas kernels for 0%

commit v1 on v0

--- a/solution.py
+++ b/solution.py
@@ -6,6 +6,7 @@
 
 H = 128
 TB = 512
+mix_the_ratios = lambda q_in: jax.lax.psum(jax.lax.psum(q_in, axis_name="cg"), axis_name="vg")
 
 
 def body(
@@ -114,7 +115,7 @@
     local_msg = jnp.dot(
         var_embed.T, grad_lin, precision=highest, preferred_element_type=jnp.float32
     )
-    grad_msg, grad_self = lax.psum((local_msg, local_self), ("cg", "vg"))
+    grad_msg, grad_self = mix_the_ratios((local_msg, local_self))
     return (con_update, grad_con, grad_var, grad_msg, grad_self)
 
 

time: 397 us -> 374 us (0.942)
  waiting for transfers between devices: 292 us -> 269 us
    psum x1 -> x2, waiting for transfers between devices: 125 us -> 101 us  [the longest x1 69.7 us: jax.lax.psum(q_in, axis_name='cg')]
    unnamed x22 -> x24, local copies, waits for them, and re-layouts: 17.9 us -> 18 us
  transfers between devices with their start and end apart: 5 -> 6, of which waited for: 5 -> 6; matrix products, arithmetic and copies ran while one was open for 5% -> 5% of each run, Pallas kernels for 0% -> 0%
where the time goes in v1:
time: 374 us; the launch traced here: 373 us
  waiting for transfers between devices  269 us (72%)
  matrix products  48.3 us (13%)
  local copies, waits for them, and re-layouts  37.5 us (10%)
  between operations  14.9 us (4%)
    reduce_scatter x1, waiting for transfers between devices, body(): lax.psum_scatter(backward_sum.reshape(col_blocks * TB, H), 'cg', scatter_...  85.6 us
    psum x1, waiting for transfers between devices, jax.lax.psum(q_in, axis_name='cg')  69.7 us
    all_gather x1, waiting for transfers between devices, body(): projected = lax.all_gather(local_proj, 'cg', axis=0, tiled=True)  48.8 us
    psum x1, waiting for transfers between devices, jax.lax.psum(jax.lax.psum(q_in, axis_name='cg'), axis_name='vg')  31.7 us
    reduce_scatter x1, waiting for transfers between devices, body(): lax.psum_scatter(forward_sum.reshape(row_blocks * TB, H), 'vg', scatter_d...  28.9 us
    unnamed x24, local copies, waits for them, and re-layouts  18 us
    dot_general x2, matrix products, backward_turn(): jnp.dot(selector, products.reshape(per_turn, TB * H), precision=highest,...  12 us
    dot_general x2, matrix products, forward_turn(): jnp.dot(selector, products.reshape(per_turn, TB * H), precision=highest,...  8.83 us
  transfers between devices with their start and end apart: 6, of which 6 were waited for; matrix products, arithmetic and copies ran while one was open for 5% of the time, Pallas kernels for 0%

profile of v1, /device:TPU:0, one launch (start us, length us, event | category | flops | bytes accessed | tf_op | source)
XLA Modules:
  0.0 373.4 jit_solution(15085152680779271917)
XLA Ops:
  8.2 2.1 fusion.31
  10.9 1.3 reduce.6
  13.7 48.8 %all-gather.3.cloned.1.call-done = bf16[8192,128]{1,0:T(8,128)(2,1)} async-done(((bf16[1024,128]{1,0:T(8,128)(2,1)}), bf16[8192,128]{1,0:T(8,128)(2,1)}) %all-gather.3.cloned.1.call-update) | async-done | bytes 2097168 | tf_op jit(solution)/shard_map/all_gather | solution.py:42
  62.5 22.9 %while.22 = (s32[]{:T(128)}, f32[8,65536]{1,0:T(8,128)}, s32[2,8]{1,0:T(2,128)S(1)}, bf16[2,8,512,512]{3,2,1,0:T(8,128)(2,1)}, s32[2,8]{1,0:T(2,128)S(1)}, /*ind...) while((s32[]{:T(128)}, f32[8,65536]{1,0:T(8,128)}, s32[2,8]{1,0:T(2,128)S(1)}, ...), condition=%wide.region_1.2_spmd.clone, body=%wide.region_0.1_spmd.clone.sunk | while | flops 588252224 | bytes 15733575 | solution.py:61
  62.5 3.2 gather_fusion
  65.8 3.7 fusion.65
  69.5 3.6 convolution_add_fusion.6
  73.2 3.2 gather_fusion
  76.4 3.7 fusion.65
  80.2 5.2 %convolution_add_fusion.6 = f32[8,65536]{1,0:T(8,128)} fusion(f32[1,8,512,128]{3,2,1,0:T(8,128)S(1)} %fusion.65, f32[8,65536]{1,0:T(8,128)} %get-tuple-element.254, pred[]{:T(512)S(6)} %compare.6, s32[8]{0:T(128)S(1)} %fusion.66), kind=kOutput, calls=%fused_computation.4.clone.1 | convolution fusion | flops 51380288 | bytes 6291489 | tf_op jit(solution)/shard_map/while/body/eval_jaxpr/dot_general | solution.py:53
  85.4 3.2 reshape.95
  89.6 28.9 %reduce-scatter.3.cloned.1.call-done = f32[1024,128]{1,0:T(8,128)} async-done(((f32[4096,128]{1,0:T(8,128)}), f32[1024,128]{1,0:T(8,128)}) %reduce-scatter.3.cloned.1.call-update) | async-done | bytes 524304 | tf_op jit(solution)/shard_map/reduce_scatter | solution.py:66
  118.5 2.9 multiply_convert_fusion
  121.5 12.3 %copy.16 = bf16[1,1,16,512,512]{3,4,2,1,0:T(8,128)(2,1)} copy(bf16[1,1,16,512,512]{4,3,2,1,0:T(8,128)(2,1)} %bitcast.88) | data formatting | bytes 16777216 | tf_op args[9]
  133.8 4.4 %all-gather.5.cloned.1.call-done = bf16[4096,128]{1,0:T(8,128)(2,1)} async-done(((bf16[1024,128]{1,0:T(8,128)(2,1)}), bf16[4096,128]{1,0:T(8,128)(2,1)}) %all-gather.5.cloned.1.call-update) | async-done | bytes 1048592 | tf_op jit(solution)/shard_map/all_gather | solution.py:87
  138.3 25.3 %while.23 = (s32[]{:T(128)}, f32[16,65536]{1,0:T(8,128)}, s32[2,8]{1,0:T(2,128)S(1)}, bf16[2,8,512,512]{2,3,1,0:T(8,128)(2,1)}, s32[2,8]{1,0:T(2,128)S(1)}, /*in...) while((s32[]{:T(128)}, f32[16,65536]{1,0:T(8,128)}, s32[2,8]{1,0:T(2,128)S(1)}, ...), condition=%wide.region_4.5_spmd.clone, body=%wide.region_3.4_spmd.clone.sunk | while | flops 639632512 | bytes 19927880 | solution.py:103
  138.3 2.9 gather_fusion.1
  141.2 3.7 fusion.71
  144.9 4.9 %convolution_add_fusion.7 = f32[16,65536]{1,0:T(8,128)} fusion(f32[16,65536]{1,0:T(8,128)} %get-tuple-element.278, f32[1,8,512,128]{3,2,1,0:T(8,128)S(1)} %fusion.71, pred[]{:T(512)S(6)} %compare.7, s32[8]{0:T(128)S(1)} %fusion.72), kind=kOutput, calls=%fused_computation.21.clone.1 | convolution fusion | flops 102760576 | bytes 10485793 | tf_op jit(solution)/shard_map/while/body/eval_jaxpr/dot_general | solution.py:95
  149.8 2.9 gather_fusion.1
  152.7 3.7 fusion.71
  156.5 7.1 %convolution_add_fusion.7 = f32[16,65536]{1,0:T(8,128)} fusion(f32[16,65536]{1,0:T(8,128)} %get-tuple-element.278, f32[1,8,512,128]{3,2,1,0:T(8,128)S(1)} %fusion.71, pred[]{:T(512)S(6)} %compare.7, s32[8]{0:T(128)S(1)} %fusion.72), kind=kOutput, calls=%fused_computation.21.clone.1 | convolution fusion | flops 102760576 | bytes 10485793 | tf_op jit(solution)/shard_map/while/body/eval_jaxpr/dot_general | solution.py:95
  163.5 3.9 %reshape.97 = f32[8192,128]{1,0:T(8,128)} reshape(f32[16,65536]{1,0:T(8,128)} %get-tuple-element.80) | data formatting | bytes 8388608 | tf_op jit(solution)/shard_map/reshape | solution.py:109
  168.6 1.7 convolution_bitcast_fusion
  170.4 85.6 %reduce-scatter.5.cloned.1.call-done = f32[1024,128]{1,0:T(8,128)} async-done(((f32[8192,128]{1,0:T(8,128)}), f32[1024,128]{1,0:T(8,128)}) %reduce-scatter.5.cloned.1.call-update) | async-done | bytes 524304 | tf_op jit(solution)/shard_map/reduce_scatter | solution.py:108
  256.0 2.9 convolution_bitcast_fusion.1
  259.0 1.5 convolution_add_fusion.2
  260.5 69.7 %all-reduce.5.cloned.1.call-done = (f32[128,128]{0,1:T(8,128)}, f32[128,128]{0,1:T(8,128)}) async-done(((f32[128,128]{0,1:T(8,128)}, f32[128,128]{0,1:T(8,128)}), (f32[128,128]{0,1:T(8,128)}, f32[128,128]{0,1:T(8,128)})) %all-reduce.5.cloned.1.call-update) | async-done | bytes 131088 | tf_op jit(solution)/shard_map/psum | solution.py:9
  330.3 1.4 fusion.33
  331.7 31.7 %all-reduce.7.cloned.1.call-done = (f32[128,128]{0,1:T(8,128)}, f32[128,128]{0,1:T(8,128)}) async-done(((f32[128,128]{0,1:T(8,128)}, f32[128,128]{0,1:T(8,128)}), (f32[128,128]{0,1:T(8,128)}, f32[128,128]{0,1:T(8,128)})) %all-reduce.7.cloned.1.call-update) | async-done | bytes 131088 | tf_op jit(solution)/shard_map/psum | solution.py:9
  363.4 1.6 copy.18
  365.0 1.6 copy.19
  (52 shorter events, 4.7 us)
Async XLA Ops:
  7.2 1.0 copy-start
  7.2 55.3 %all-gather.3.cloned.1.call-start = ((), (), s32[]{:S(2)}) async-start(), calls=%async_computation.2 | async-start | bytes 2359296 | tf_op jit(solution)/shard_map/all_gather | solution.py:42
  10.3 108.2 %reduce-scatter.3.cloned.1.call-start = ((), (), s32[]{:S(2)}) async-start(), calls=%async_computation.3 | async-start | bytes 2621440 | tf_op jit(solution)/shard_map/reduce_scatter | solution.py:66
  88.6 29.9 %copy-start.4 = (f32[1024,128]{1,0:T(8,128)S(1)}, f32[1024,128]{1,0:T(8,128)}, u32[]{:S(2)}) copy-start(f32[1024,128]{1,0:T(8,128)} %param.15) | copy-start | bytes 1572868
  88.6 29.9 %copy-start.5 = (f32[1024,128]{1,0:T(8,128)S(1)}, f32[1024,128]{1,0:T(8,128)}, u32[]{:S(2)}) copy-start(f32[1024,128]{1,0:T(8,128)} %param.25) | copy-start | bytes 1572868
  88.6 29.9 %copy-start.7 = (f32[128,128]{1,0:T(8,128)S(1)}, f32[128,128]{1,0:T(8,128)}, u32[]{:S(2)}) copy-start(f32[128,128]{1,0:T(8,128)} %param.19) | copy-start | bytes 196612
  88.6 29.9 %copy-start.8 = (f32[1024]{0:T(1024)S(1)}, f32[1024]{0:T(1024)}, u32[]{:S(2)}) copy-start(f32[1024]{0:T(1024)} %param.17) | copy-start | bytes 12292
  88.7 49.6 %all-gather.5.cloned.1.call-start = ((), (), s32[]{:S(2)}) async-start(), calls=%async_computation.4 | async-start | bytes 1310720 | tf_op jit(solution)/shard_map/all_gather | solution.py:87
  121.4 134.5 %reduce-scatter.5.cloned.1.call-start = ((), (), s32[]{:S(2)}) async-start(), calls=%async_computation.5 | async-start | bytes 4718592 | tf_op jit(solution)/shard_map/reduce_scatter | solution.py:108
  167.4 1.0 copy-start.6
  167.4 1.2 copy-start.9
  167.4 88.5 %copy-start.3 = (f32[1024]{0:T(1024)S(1)}, f32[1024]{0:T(1024)}, u32[]{:S(2)}) copy-start(f32[1024]{0:T(1024)} %param.18) | copy-start | bytes 12292
  167.4 162.8 %all-reduce.5.cloned.1.call-start = ((), (), s32[]{:S(2)}) async-start(), calls=%async_computation.6 | async-start | bytes 262144 | tf_op jit(solution)/shard_map/psum | solution.py:9
  170.3 159.9 %copy-start.2 = (f32[128,128]{1,0:T(8,128)S(1)}, f32[128,128]{1,0:T(8,128)}, u32[]{:S(2)}) copy-start(f32[128,128]{1,0:T(8,128)} %param.20) | copy-start | bytes 196612
  256.0 74.3 %copy-start.1 = (f32[1024,128]{1,0:T(8,128)S(1)}, f32[1024,128]{1,0:T(8,128)}, u32[]{:S(2)}) copy-start(f32[1024,128]{1,0:T(8,128)} %reduce-scatter.5.cloned.1.call-done) | copy-start | bytes 1572868
  258.9 104.5 %all-reduce.7.cloned.1.call-start = ((), (), s32[]{:S(2)}) async-start(), calls=%async_computation.7 | async-start | bytes 262144 | tf_op jit(solution)/shard_map/psum | solution.py:9
Sparse Core Ops, SparseCore 0:
  10.7 51.7 all-gather.2
  88.8 29.6 reduce-scatter.2
  121.5 16.6 all-gather.4
  167.6 88.3 reduce-scatter.4
  259.9 70.3 all-reduce.4
  332.5 30.9 all-reduce.6
